TPU v7x, 32 devices: a whole 2x2x4 slice. The times are simulated.
32 devices in a mesh: slides: 2 (over y), rows: 4 (over z), cols: 2 (over x), chan: 2 (over core).
Axes of the slice: x: 2, y: 2, z: 4, core: 2. Of those that a mesh axis runs over, the one named last changes fastest.
Arguments:
- features: bfloat16 [128, 64, 384], P(('slides', 'rows'), 'cols', 'chan'), parts along dimension 0, may hold values from -6 to 6
- gate_input: bfloat16 [128, 64, 384], P(('slides', 'rows'), 'cols', 'chan'), parts along dimension 0, may hold values from -6 to 6
- decay_idx: int32 [128, 64], P(('slides', 'rows'), 'cols'), parts along dimension 0, may hold values from 0 to 15
- log_table: float32 [16, 384], P(None, 'chan'), may hold values from -1 to 0, as said below
- state_rate: float32 [16], replicated, may hold values from 0.5 to 2
- proj_row: bfloat16 [384, 32], P('chan'), may hold values from -0.0390625 to 0.0390625
- proj_col: bfloat16 [384, 32], P('chan'), may hold values from -0.0390625 to 0.0390625
- conv_w: float32 [3, 3, 384], P(None, None, 'chan'), may hold values from -0.5 to 0.5
- conv_b: float32 [384], P('chan'), may hold values from -0.5 to 0.5
- d_skip: float32 [384], P('chan'), may hold values from 0.5 to 1.5
Outputs:
- output: bfloat16 [128, 64, 384], P(('slides', 'rows'), 'cols', 'chan'), parts along dimension 0
There are 2 independent parts, one for each index of `slides`. A program takes and returns all parts, laid end to end along the dimension named above; an argument that names none is the same for every part. Nothing has to cross between parts.
Inputs may be any that keep to these rules, and one draw needn't show every extreme that they name: `log_table`: every entry is negative.
All inputs are finite; a program needn't handle non-finite values.
Results may differ from a plain program's by a relative error of at most 0.0061.
Values may be sent and summed in bfloat16 or wider, within the bound.
No kernel may reach another device: no remote copies, remote signals or barrier semaphores. Data moves between devices by JAX's collectives and lax.ppermute only.
A program may use at most 128 MiB of HBM per device.

v0:
```python
import jax
import jax.numpy as jnp
from jax import lax
from jax.sharding import PartitionSpec as P


def entering(shard, axis, combine, identity):
    size, position = (lax.axis_size(axis), lax.axis_index(axis))
    everything = jax.tree.map(lambda part: lax.all_gather(part, axis), shard)
    start = jax.tree.map(
        lambda part, zero: jnp.broadcast_to(jnp.asarray(zero, part.dtype), part.shape),
        shard,
        identity,
    )

    def step(k, before):
        reached = k < position
        new = combine(before, jax.tree.map(lambda part: part[k], everything))
        return jax.tree.map(lambda a, b: jnp.where(reached, a, b), new, before)

    return lax.fori_loop(0, size, step, start)


def extended(block, sides, width):
    for axis, dim in sides:
        count = lax.axis_size(axis)
        forward = [(i, i + 1) for i in range(count - 1)]
        backward = [(target, source) for source, target in forward]
        low = lax.ppermute(
            lax.slice_in_dim(block, block.shape[dim] - width, None, axis=dim), axis, forward
        )
        high = lax.ppermute(lax.slice_in_dim(block, 0, width, axis=dim), axis, backward)
        block = jnp.concatenate([low, block, high], axis=dim)
    return block


def combine_pair(earlier, latter):
    return (earlier[0] + latter[0], latter[1] + jnp.exp(latter[0]) * earlier[1])


def make_carry_combine(state_rate):
    rates = state_rate[:, None, None]

    def combine_carry(earlier, latter):
        return (earlier[0] + latter[0], latter[1] + jnp.exp(rates * latter[0][None]) * earlier[1])

    return combine_carry


def lookup(decay_idx, log_table):
    entries = log_table.shape[0]
    onehot = (decay_idx[..., None] == jnp.arange(entries, dtype=jnp.int32)).astype(jnp.float32)
    return jnp.einsum("hwk,ke->hwe", onehot, log_table, precision=lax.Precision.HIGHEST)


def tile_states(values, log_decays, coeffs, state_rate, scan_axis):
    num_states = state_rate.shape[0]
    drive_cols = jnp.moveaxis(coeffs[..., :num_states], -1, 0)[..., None]
    log_sums = jnp.cumsum(log_decays, axis=scan_axis)

    def one_state(inputs):
        state_scale, drive_col = inputs
        unused, states = lax.associative_scan(
            combine_pair, (log_decays * state_scale, drive_col * values), axis=scan_axis
        )
        return states

    return (log_sums, lax.map(one_state, (state_rate, drive_cols)))


def finish(log_sums, states, inflow, coeffs, state_rate):
    num_states = states.shape[0]
    outputs = jnp.moveaxis(coeffs[..., num_states:], -1, 0)[..., None]
    carried = jnp.exp(state_rate[:, None, None, None] * log_sums[None]) * inflow
    return jnp.sum(outputs * (states + carried), axis=0)


def column_coeffs(middle, proj_col):
    return lax.psum(jnp.dot(middle, proj_col, preferred_element_type=jnp.float32), "chan")


def shards(
    features,
    gate_input,
    decay_idx,
    log_table,
    state_rate,
    proj_row,
    proj_col,
    conv_w,
    conv_b,
    d_skip,
):
    combine_carry = make_carry_combine(state_rate)
    log_decays = lookup(decay_idx, log_table)
    feats_wide = features.astype(jnp.float32)
    coeff_row = lax.psum(jnp.dot(features, proj_row, preferred_element_type=jnp.float32), "chan")
    row_sums, states = tile_states(feats_wide, log_decays, coeff_row, state_rate, 1)
    tile_ends = (row_sums[:, -1, :], states[:, :, -1, :])
    incoming = entering(
        tile_ends,
        "cols",
        combine_carry,
        (jnp.zeros_like(tile_ends[0]), jnp.zeros_like(tile_ends[1])),
    )
    swept_rows = finish(row_sums, states, incoming[1][:, :, None, :], coeff_row, state_rate)
    row_out = (swept_rows + d_skip * feats_wide).astype(jnp.bfloat16)
    padded = extended(row_out, (("rows", 0), ("cols", 1)), 1).astype(jnp.float32)
    tile_rows = row_out.shape[0]
    tile_cols = row_out.shape[1]
    convolved = jnp.zeros(row_out.shape, jnp.float32) + conv_b
    for offset_row in range(3):
        for offset_col in range(3):
            convolved = (
                convolved
                + conv_w[offset_row, offset_col]
                * padded[offset_row : offset_row + tile_rows, offset_col : offset_col + tile_cols]
            )
    middle = jax.nn.silu(convolved).astype(jnp.bfloat16)
    strip_vals = lax.all_to_all(middle, "rows", split_axis=1, concat_axis=0, tiled=True)
    strip_index = lax.all_to_all(decay_idx, "rows", split_axis=1, concat_axis=0, tiled=True)
    strip_decays = lookup(strip_index, log_table)
    strip_wide = strip_vals.astype(jnp.float32)
    coeff_col = column_coeffs(strip_vals, proj_col)
    col_sums, states = tile_states(strip_wide, strip_decays, coeff_col, state_rate, 0)
    strip_out = (
        finish(col_sums, states, jnp.zeros((), jnp.float32), coeff_col, state_rate)
        + d_skip * strip_wide
    )
    combined = lax.all_to_all(strip_out, "rows", split_axis=0, concat_axis=1, tiled=True)
    return (combined * jax.nn.silu(gate_input.astype(jnp.float32))).astype(jnp.bfloat16)


def solution(mesh):
    placed = (
        P(("slides", "rows"), "cols", "chan"),
        P(("slides", "rows"), "cols", "chan"),
        P(("slides", "rows"), "cols"),
        P(None, "chan"),
        P(),
        P("chan", None),
        P("chan", None),
        P(None, None, "chan"),
        P("chan"),
        P("chan"),
    )
    return jax.shard_map(
        shards,
        mesh=mesh,
        in_specs=placed,
        out_specs=P(("slides", "rows"), "cols", "chan"),
        check_vma=False,
    )
```

profile of v0, /device:TPU:0, one launch (start us, length us, event | category | flops | bytes accessed | tf_op | source)
XLA Modules:
  0.0 399.4 jit_solution(8053558625621068115)
XLA Ops:
  6.5 1.9 fusion.42
  9.9 6.3 %all-to-all-start.1 = ((s32[4,1,128]{2,1,0:T(1,128)}), s32[4,1,128]{2,1,0:T(1,128)S(1)}, u32[]{:S(2)}, u32[]{:S(2)}) async-start(s32[4,1,128]{2,1,0:T(1,128)} %reshape.23), calls=%async_computation.1 | async-start | bytes 4096 | tf_op jit(solution)/shard_map/all_to_all | solution.py:121
  20.7 4.4 %all-gather.1 = f32[32,1,192]{2,0,1:T(8,128)S(1)} all-gather(f32[16,1,192]{2,0,1:T(8,128)S(1)} %slice.400), channel_id=3, replica_groups=mesh['slides'=2,'rows'=4,'cols'=2,'chan'=2] {'cols'}, dimensions={0}, use_global_device_ids=true | all-gather | bytes 36864 | tf_op jit(solution)/shard_map/all_gather | solution.py:9
  25.1 5.5 %all-reduce.25.cloned.1.call-done = f32[16,32,32]{2,1,0:T(8,128)} async-done(((f32[16,32,32]{2,1,0:T(8,128)}), f32[16,32,32]{2,1,0:T(8,128)}) %all-reduce.25.cloned.1.call-update) | async-done | bytes 65552 | tf_op jit(solution)/shard_map/psum | solution.py:97
  30.6 1.9 slice_bitcast_fusion.3
  33.3 179.7 %while.37 = (s32[]{:T(128)}, f32[16,16,32,192]{3,2,1,0:T(8,128)}, f32[16,16,32,1]{2,1,3,0:T(8,128)}, f32[16,32,192]{2,1,0:T(8,128)}, f32[16]{0:T(128)}, /*index=5*/f32[16,32,192]{2,1,0:T(8,128)S(1)}) while((s32[]{:T(128)}, f32[16,16,32,192]{3,2,1,0:T(8,128)}, f32[16,16,32,1]{2,1,3,0:T(8,128)}, f32[16,32,192]{2,1,0:T(8,128)}, ...), condition=%wide.region_2.3_spmd.clone, body=%wide.region_1.0_spmd.sunk.clone | while | flops 998402 | bytes 15030905 | solution.py:68
  35.3 1.9 broadcast_multiply_fusion.8
  46.5 1.9 broadcast_multiply_fusion.8
  136.3 1.9 broadcast_multiply_fusion.8
  192.4 1.9 broadcast_multiply_fusion.8
  212.9 9.9 %copy.50 = f32[16,16,32,192]{3,1,2,0:T(8,128)S(1)} copy(f32[16,16,32,192]{3,2,1,0:T(8,128)} %get-tuple-element.178) | data formatting | bytes 12582912 | tf_op jit(solution)/shard_map/while | solution.py:68
  223.0 9.5 %all-gather = f32[32,16,1,192]{3,1,2,0:T(8,128)S(1)} all-gather(f32[16,16,1,192]{3,1,2,0:T(8,128)S(1)} %slice.399), channel_id=2, replica_groups=mesh['slides'=2,'rows'=4,'cols'=2,'chan'=2] {'cols'}, dimensions={0}, use_global_device_ids=true | all-gather | bytes 589824 | tf_op jit(solution)/shard_map/all_gather | solution.py:9
  232.9 4.8 %multiply_reduce_fusion.1 = f32[16,32,192]{2,1,0:T(8,128)S(1)} fusion(f32[16,16,32,192]{3,2,1,0:T(8,128)} %get-tuple-element.178, f32[16,16,192]{2,1,0:T(8,128)S(1)} %get-tuple-element.179, f32[16,32,192]{2,1,0:T(8,128)S(1)} %copy-done.4, f32[16]{0:T(128)S(1)} %bitcast.166, f32[16,16,32]{2,1,0:T(8,128)S(1)} %copy.46), kind=kLoop, calls=%fused_computation.70 | loop fusion | flops 7766016 | bytes 7307328 | tf_op jit(solution)/shard_map/reduce_sum | solution.py:75
  237.9 3.7 collective-permute-start
  244.2 3.0 collective-permute-done.1
  247.2 3.4 collective-permute-start.2
  252.0 4.2 %collective-permute-done.3 = bf16[18,1,192]{2,1,0:T(2,128)(2,1)S(1)} collective-permute-done((bf16[18,1,192]{2,1,0:T(2,128)(2,1)S(1)}, bf16[18,1,192]{2,1,0:T(2,128)(2,1)S(1)}, u32[]{:S(2)}, u32[]{:S(2)}) %collective-permute-start.3) | collective-permute-done | bytes 6944 | tf_op jit(solution)/shard_map/ppermute | solution.py:32
  257.8 3.7 all-to-all-start
  262.8 5.4 %all-to-all-done = bf16[16,32,192]{2,0,1:T(8,128)(2,1)S(1)} async-done(((bf16[16,32,192]{2,0,1:T(8,128)(2,1)}), bf16[16,32,192]{2,0,1:T(8,128)(2,1)S(1)}, u32[]{:S(2)}, u32[]{:S(2)}) %all-to-all-start) | async-done | bytes 196640 | tf_op jit(solution)/shard_map/all_to_all | solution.py:120
  269.3 17.2 %all-reduce.27.cloned.1.call-done = f32[64,8,32]{2,1,0:T(8,128)} async-done(((f32[64,8,32]{2,1,0:T(8,128)}), f32[64,8,32]{2,1,0:T(8,128)}) %all-reduce.27.cloned.1.call-update) | async-done | bytes 65552 | tf_op jit(solution)/shard_map/psum | solution.py:79
  286.5 1.9 slice_bitcast_fusion.1
  289.6 76.2 %while.38 = (s32[]{:T(128)}, f32[16,64,8,192]{3,2,1,0:T(8,128)}, f32[16,64,8,1]{2,1,3,0:T(8,128)}, f32[64,8,192]{2,1,0:T(8,128)S(1)}, f32[16]{0:T(128)S(1)}, /*index=5*/f32[64,8,192]{2,1,0:T(8,128)S(1)}) while((s32[]{:T(128)}, f32[16,64,8,192]{3,2,1,0:T(8,128)}, f32[16,64,8,1]{2,1,3,0:T(8,128)}, f32[64,8,192]{2,1,0:T(8,128)S(1)}, ...), condition=%wide.region_9.10_spmd.clone, body=%wide.region_8.9_spmd.sunk.clone | while | flops 1035266 | bytes 11215489 | solution.py:68
  367.3 4.7 %multiply_reduce_fusion = f32[64,8,192]{2,1,0:T(8,128)S(1)} fusion(f32[16,64,8,192]{3,2,1,0:T(8,128)} %get-tuple-element.180, f32[64,8,192]{2,1,0:T(8,128)} %fusion.52, f32[16]{0:T(128)S(1)} %get-tuple-element.646, f32[16,64,8]{2,1,0:T(8,128)S(1)} %copy.53), kind=kLoop, calls=%fused_computation.69 | loop fusion | flops 7766016 | bytes 7110720 | tf_op jit(solution)/shard_map/reduce_sum | solution.py:75
  372.1 19.6 %all_to_all.52 = f32[64,8,192]{2,1,0:T(8,128)S(1)} all-to-all(f32[64,8,192]{2,1,0:T(8,128)S(1)} %multiply_add_fusion.9), channel_id=1, replica_groups=mesh['slides'=2,'rows'=4,'cols'=2,'chan'=2] {'rows'}, dimensions={0} | all-to-all | bytes 786432 | tf_op jit(solution)/shard_map/all_to_all | solution.py:130
  (1557 shorter events, 257.6 us)
Async XLA Ops:
  6.5 9.7 %copy-start = (f32[16,192]{1,0:T(8,128)S(1)}, f32[16,192]{1,0:T(8,128)}, u32[]{:S(2)}) copy-start(f32[16,192]{1,0:T(8,128)} %param.19) | copy-start | bytes 36868
  6.5 24.1 %all-reduce.25.cloned.1.call-start = ((), (), s32[]{:S(2)}) async-start(), calls=%async_computation.3 | async-start | bytes 524288 | tf_op jit(solution)/shard_map/psum | solution.py:97
  9.9 233.0 %all-to-all-start.1 = ((s32[4,1,128]{2,1,0:T(1,128)}), s32[4,1,128]{2,1,0:T(1,128)S(1)}, u32[]{:S(2)}, u32[]{:S(2)}) async-start(s32[4,1,128]{2,1,0:T(1,128)} %reshape.23), calls=%async_computation.1 | async-start | bytes 4096 | tf_op jit(solution)/shard_map/all_to_all | solution.py:121
  212.9 19.5 %copy-start.7 = (f32[16]{0:T(128)S(1)}, f32[16]{0:T(128)}, u32[]{:S(2)}) copy-start(f32[16]{0:T(128)} %get-tuple-element.644) | copy-start | bytes 196
  212.9 19.8 %copy-start.5 = (f32[16,16,32]{0,2,1:T(8,128)S(1)}, f32[16,16,32]{0,2,1:T(8,128)}, u32[]{:S(2)}) copy-start(f32[16,16,32]{0,2,1:T(8,128)} %get-tuple-element.321) | copy-start | bytes 98308
  212.9 20.0 %copy-start.4 = (f32[16,32,192]{2,1,0:T(8,128)S(1)}, f32[16,32,192]{2,1,0:T(8,128)}, u32[]{:S(2)}) copy-start(f32[16,32,192]{2,1,0:T(8,128)} %copy.49) | copy-start | bytes 1179652
  222.9 14.9 %copy-start.3 = (bf16[16,32,192]{2,1,0:T(8,128)(2,1)S(1)}, bf16[16,32,192]{2,1,0:T(8,128)(2,1)}, u32[]{:S(2)}) copy-start(bf16[16,32,192]{2,1,0:T(8,128)(2,1)} %param.16) | copy-start | bytes 589828
  222.9 14.9 %copy-start.10 = (f32[192]{0:T(256)S(1)}, f32[192]{0:T(256)}, u32[]{:S(2)}) copy-start(f32[192]{0:T(256)} %param.25) | copy-start | bytes 2308
  222.9 19.9 %copy-start.9 = (f32[3,3,192]{2,1,0:T(4,128)S(1)}, f32[3,3,192]{2,1,0:T(4,128)}, u32[]{:S(2)}) copy-start(f32[3,3,192]{2,1,0:T(4,128)} %param.23) | copy-start | bytes 20740
  232.4 24.0 %copy-start.11 = (f32[192]{0:T(256)S(1)}, f32[192]{0:T(256)}, u32[]{:S(2)}) copy-start(f32[192]{0:T(256)} %param.24) | copy-start | bytes 2308
  232.9 35.4 %copy-start.8 = (bf16[192,32]{0,1:T(8,128)(2,1)S(1)}, bf16[192,32]{0,1:T(8,128)(2,1)}, u32[]{:S(2)}) copy-start(bf16[192,32]{0,1:T(8,128)(2,1)} %param.22) | copy-start | bytes 36868
  237.9 6.3 %collective-permute-start = (bf16[1,32,192]{2,1,0:T(8,128)(2,1)S(1)}, bf16[1,32,192]{2,1,0:T(8,128)(2,1)S(1)}, u32[]{:S(2)}, u32[]{:S(2)}) collective-permute-start(bf16[1,32,192]{2,1,0:T(8,128)(2,1)S(1)} %get-tuple-element.319), channel_id=1, source_target_pairs={{0,4},{4,8},{8,12},{1,5},{5,9},{9,13},{2,6},{6,10},{10,14},{3,7},{... | collective-permute-start | bytes 36872 | tf_op jit(solution)/shard_map/ppermute | solution.py:29
  241.5 5.6 %collective-permute-start.1 = (bf16[1,32,192]{2,1,0:T(8,128)(2,1)S(1)}, bf16[1,32,192]{2,1,0:T(8,128)(2,1)S(1)}, u32[]{:S(2)}, u32[]{:S(2)}) collective-permute-start(bf16[1,32,192]{2,1,0:T(8,128)(2,1)S(1)} %get-tuple-element.320), channel_id=1, source_target_pairs={{4,0},{8,4},{12,8},{5,1},{9,5},{13,9},{6,2},{10,6},{14,10},{7,3},{... | collective-permute-start | bytes 36872 | tf_op jit(solution)/shard_map/ppermute | solution.py:32
  247.2 4.8 %collective-permute-start.2 = (bf16[18,1,192]{2,1,0:T(2,128)(2,1)S(1)}, bf16[18,1,192]{2,1,0:T(2,128)(2,1)S(1)}, u32[]{:S(2)}, u32[]{:S(2)}) collective-permute-start(bf16[18,1,192]{2,1,0:T(2,128)(2,1)S(1)} %get-tuple-element.315), channel_id=1, source_target_pairs={{0,2},{1,3},{4,6},{5,7},{8,10},{9,11},{12,14},{13,15},{16,18},{17,... | collective-permute-start | bytes 20744 | tf_op jit(solution)/shard_map/ppermute | solution.py:29
  250.6 5.7 %collective-permute-start.3 = (bf16[18,1,192]{2,1,0:T(2,128)(2,1)S(1)}, bf16[18,1,192]{2,1,0:T(2,128)(2,1)S(1)}, u32[]{:S(2)}, u32[]{:S(2)}) collective-permute-start(bf16[18,1,192]{2,1,0:T(2,128)(2,1)S(1)} %get-tuple-element.316), channel_id=1, source_target_pairs={{2,0},{3,1},{6,4},{7,5},{10,8},{11,9},{14,12},{15,13},{18,16},{19,... | collective-permute-start | bytes 20744 | tf_op jit(solution)/shard_map/ppermute | solution.py:32
  257.8 10.5 %all-to-all-start = ((bf16[16,32,192]{2,0,1:T(8,128)(2,1)}), bf16[16,32,192]{2,0,1:T(8,128)(2,1)S(1)}, u32[]{:S(2)}, u32[]{:S(2)}) async-start(bf16[16,32,192]{2,0,1:T(8,128)(2,1)} %copy.51), calls=%async_computation | async-start | bytes 524288 | tf_op jit(solution)/shard_map/all_to_all | solution.py:120
  261.4 25.0 %all-reduce.27.cloned.1.call-start = ((), (), s32[]{:S(2)}) async-start(), calls=%async_computation.4 | async-start | bytes 524288 | tf_op jit(solution)/shard_map/psum | solution.py:79
  268.3 21.3 %copy-start.1 = (bf16[16,4,8,192]{3,2,0,1:T(8,128)(2,1)}, bf16[16,4,8,192]{3,2,0,1:T(8,128)(2,1)S(1)}, u32[]{:S(2)}) copy-start(bf16[16,4,8,192]{3,2,0,1:T(8,128)(2,1)S(1)} %copy.52) | copy-start | bytes 589828
  365.8 6.2 %copy-start.2 = (bf16[16,4,8,192]{3,2,0,1:T(8,128)(2,1)S(1)}, bf16[16,4,8,192]{3,2,0,1:T(8,128)(2,1)}, u32[]{:S(2)}) copy-start(bf16[16,4,8,192]{3,2,0,1:T(8,128)(2,1)} %copy-done.1) | copy-start | bytes 589828
  365.8 25.9 %copy-start.6 = (bf16[16,32,192]{2,1,0:T(8,128)(2,1)S(1)}, bf16[16,32,192]{2,1,0:T(8,128)(2,1)}, u32[]{:S(2)}) copy-start(bf16[16,32,192]{2,1,0:T(8,128)(2,1)} %param.17) | copy-start | bytes 589828
Sparse Core Ops, SparseCore 0:
  9.7 20.9 all-reduce.24
  269.4 17.0 all-reduce.26
where the time goes:
time: 403 us; the launch traced here: 399 us
  local copies, waits for them, and re-layouts  178 us (44%)
  other arithmetic  104 us (26%)
  waiting for transfers between devices  35.4 us (9%)
  blocking collectives  33.5 us (8%)
  starting transfers between devices  19.6 us (5%)
  between operations  13.7 us (3%)
  loops' own time  10.1 us (3%)
  matrix products  4.34 us (1%)
    slice x464, local copies, waits for them, and re-layouts, one_state(): lax.associative_scan(combine_pair, (log_decays * state_scale, drive_col *...  66 us
    mul x32, other arithmetic, one_state(): log_decays * state_scale  41.8 us
    pad x288, local copies, waits for them, and re-layouts, one_state(): lax.associative_scan(combine_pair, (log_decays * state_scale, drive_col *...  36.8 us
    dynamic_slice x32, local copies, waits for them, and re-layouts, tile_states(): return (log_sums, lax.map(one_state, (state_rate, drive_cols)))  30.6 us
    dynamic_update_slice x32, other arithmetic, tile_states(): return (log_sums, lax.map(one_state, (state_rate, drive_cols)))  28.1 us
    mul x32, local copies, waits for them, and re-layouts, one_state(): drive_col * values  23.3 us
    all_to_all x1, blocking collectives, shards(): lax.all_to_all(strip_out, 'rows', split_axis=0, concat_axis=1, tiled=True)  19.6 us
    psum x1, waiting for transfers between devices, column_coeffs(): lax.psum(jnp.dot(middle, proj_col, preferred_element_type=jnp.float32), '...  17.2 us
  transfers between devices with their start and end apart: 8, of which 6 were waited for; matrix products, arithmetic and copies ran while one was open for 50% of the time, Pallas kernels for 0%

commit v1 on v0

--- a/solution.py
+++ b/solution.py
@@ -127,7 +127,12 @@
         finish(col_sums, states, jnp.zeros((), jnp.float32), coeff_col, state_rate)
         + d_skip * strip_wide
     )
-    combined = lax.all_to_all(strip_out, "rows", split_axis=0, concat_axis=1, tiled=True)
+    combined = jnp.concatenate(
+        lax.all_to_all(
+            jnp.stack(jnp.split(strip_out, lax.axis_size("rows"), axis=0)), "rows", 0, 0
+        ),
+        axis=1,
+    )
     return (combined * jax.nn.silu(gate_input.astype(jnp.float32))).astype(jnp.bfloat16)
 
 

time: 403 us -> 404 us (level)
  no operation moved by 1% of the time
where the time goes in v1:
time: 404 us; the launch traced here: 401 us
  local copies, waits for them, and re-layouts  179 us (44%)
  other arithmetic  105 us (26%)
  waiting for transfers between devices  35.4 us (9%)
  blocking collectives  33.5 us (8%)
  starting transfers between devices  19.6 us (5%)
  between operations  13.7 us (3%)
  loops' own time  10.1 us (2%)
  matrix products  4.34 us (1%)
    slice x464, local copies, waits for them, and re-layouts, one_state(): lax.associative_scan(combine_pair, (log_decays * state_scale, drive_col *...  66 us
    mul x32, other arithmetic, one_state(): log_decays * state_scale  42.3 us
    pad x288, local copies, waits for them, and re-layouts, one_state(): lax.associative_scan(combine_pair, (log_decays * state_scale, drive_col *...  36.8 us
    dynamic_slice x32, local copies, waits for them, and re-layouts, tile_states(): return (log_sums, lax.map(one_state, (state_rate, drive_cols)))  31.2 us
    dynamic_update_slice x32, other arithmetic, tile_states(): return (log_sums, lax.map(one_state, (state_rate, drive_cols)))  28.4 us
    mul x32, local copies, waits for them, and re-layouts, one_state(): drive_col * values  23.3 us
    all_to_all x1, blocking collectives, shards(): lax.all_to_all(jnp.stack(jnp.split(strip_out, lax.axis_size('rows'), axis...  19.6 us
    psum x1, waiting for transfers between devices, column_coeffs(): lax.psum(jnp.dot(middle, proj_col, preferred_element_type=jnp.float32), '...  17.2 us
  transfers between devices with their start and end apart: 8, of which 6 were waited for; matrix products, arithmetic and copies ran while one was open for 50% of the time, Pallas kernels for 0%

profile of v1, /device:TPU:0, one launch (start us, length us, event | category | flops | bytes accessed | tf_op | source)
XLA Modules:
  0.0 400.9 jit_solution(7545759124729001668)
XLA Ops:
  6.5 1.9 fusion.42
  9.9 6.3 %all-to-all-start.1 = ((s32[4,1,128]{2,1,0:T(1,128)}), s32[4,1,128]{2,1,0:T(1,128)S(1)}, u32[]{:S(2)}, u32[]{:S(2)}) async-start(s32[4,1,128]{2,1,0:T(1,128)} %reshape.31), calls=%async_computation.1 | async-start | bytes 4096 | tf_op jit(solution)/shard_map/all_to_all | solution.py:121
  20.7 4.4 %all-gather.1 = f32[32,1,192]{2,0,1:T(8,128)S(1)} all-gather(f32[16,1,192]{2,0,1:T(8,128)S(1)} %slice.400), channel_id=3, replica_groups=mesh['slides'=2,'rows'=4,'cols'=2,'chan'=2] {'cols'}, dimensions={0}, use_global_device_ids=true | all-gather | bytes 36864 | tf_op jit(solution)/shard_map/all_gather | solution.py:9
  25.1 5.5 %all-reduce.25.cloned.1.call-done = f32[16,32,32]{2,1,0:T(8,128)} async-done(((f32[16,32,32]{2,1,0:T(8,128)}), f32[16,32,32]{2,1,0:T(8,128)}) %all-reduce.25.cloned.1.call-update) | async-done | bytes 65552 | tf_op jit(solution)/shard_map/psum | solution.py:97
  30.6 1.9 slice_bitcast_fusion.3
  33.3 179.4 %while.37 = (s32[]{:T(128)}, f32[16,16,32,192]{3,2,1,0:T(8,128)}, f32[16,16,32,1]{2,1,3,0:T(8,128)}, f32[16,32,192]{2,1,0:T(8,128)}, f32[16]{0:T(128)}, /*index=5*/f32[16,32,192]{2,1,0:T(8,128)S(1)}) while((s32[]{:T(128)}, f32[16,16,32,192]{3,2,1,0:T(8,128)}, f32[16,16,32,1]{2,1,3,0:T(8,128)}, f32[16,32,192]{2,1,0:T(8,128)}, ...), condition=%wide.region_2.3_spmd.clone, body=%wide.region_1.0_spmd.sunk.clone | while | flops 998402 | bytes 15030905 | solution.py:68
  102.5 1.8 broadcast_multiply_fusion.8
  124.9 1.8 broadcast_multiply_fusion.8
  147.4 1.8 broadcast_multiply_fusion.8
  169.8 1.8 broadcast_multiply_fusion.8
  212.7 9.9 %copy.33 = f32[16,16,32,192]{3,1,2,0:T(8,128)S(1)} copy(f32[16,16,32,192]{3,2,1,0:T(8,128)} %get-tuple-element.178) | data formatting | bytes 12582912 | tf_op jit(solution)/shard_map/while | solution.py:68
  222.7 9.5 %all-gather = f32[32,16,1,192]{3,1,2,0:T(8,128)S(1)} all-gather(f32[16,16,1,192]{3,1,2,0:T(8,128)S(1)} %slice.399), channel_id=2, replica_groups=mesh['slides'=2,'rows'=4,'cols'=2,'chan'=2] {'cols'}, dimensions={0}, use_global_device_ids=true | all-gather | bytes 589824 | tf_op jit(solution)/shard_map/all_gather | solution.py:9
  232.7 4.8 %multiply_reduce_fusion.1 = f32[16,32,192]{2,1,0:T(8,128)S(1)} fusion(f32[16,16,32,192]{3,2,1,0:T(8,128)} %get-tuple-element.178, f32[16,16,192]{2,1,0:T(8,128)S(1)} %get-tuple-element.179, f32[16,32,192]{2,1,0:T(8,128)S(1)} %copy-done.4, f32[16]{0:T(128)S(1)} %bitcast.173, f32[16,16,32]{2,1,0:T(8,128)S(1)} %copy.29), kind=kLoop, calls=%fused_computation.70 | loop fusion | flops 7766016 | bytes 7307328 | tf_op jit(solution)/shard_map/reduce_sum | solution.py:75
  237.6 3.7 collective-permute-start
  243.9 3.0 collective-permute-done.1
  247.0 3.4 collective-permute-start.2
  251.8 4.2 %collective-permute-done.3 = bf16[18,1,192]{2,1,0:T(2,128)(2,1)S(1)} collective-permute-done((bf16[18,1,192]{2,1,0:T(2,128)(2,1)S(1)}, bf16[18,1,192]{2,1,0:T(2,128)(2,1)S(1)}, u32[]{:S(2)}, u32[]{:S(2)}) %collective-permute-start.3) | collective-permute-done | bytes 6944 | tf_op jit(solution)/shard_map/ppermute | solution.py:32
  257.5 3.7 all-to-all-start
  262.6 5.4 %all-to-all-done = bf16[16,32,192]{2,0,1:T(8,128)(2,1)S(1)} async-done(((bf16[16,32,192]{2,0,1:T(8,128)(2,1)}), bf16[16,32,192]{2,0,1:T(8,128)(2,1)S(1)}, u32[]{:S(2)}, u32[]{:S(2)}) %all-to-all-start) | async-done | bytes 196640 | tf_op jit(solution)/shard_map/all_to_all | solution.py:120
  269.1 17.2 %all-reduce.27.cloned.1.call-done = f32[64,8,32]{2,1,0:T(8,128)} async-done(((f32[64,8,32]{2,1,0:T(8,128)}), f32[64,8,32]{2,1,0:T(8,128)}) %all-reduce.27.cloned.1.call-update) | async-done | bytes 65552 | tf_op jit(solution)/shard_map/psum | solution.py:79
  286.2 1.9 slice_bitcast_fusion.1
  289.3 77.8 %while.38 = (s32[]{:T(128)}, f32[16,64,8,192]{3,2,1,0:T(8,128)}, f32[16,64,8,1]{2,1,3,0:T(8,128)}, f32[64,8,192]{2,1,0:T(8,128)S(1)}, f32[16]{0:T(128)S(1)}, /*index=5*/f32[64,8,192]{2,1,0:T(8,128)S(1)}) while((s32[]{:T(128)}, f32[16,64,8,192]{3,2,1,0:T(8,128)}, f32[16,64,8,1]{2,1,3,0:T(8,128)}, f32[64,8,192]{2,1,0:T(8,128)S(1)}, ...), condition=%wide.region_9.10_spmd.clone, body=%wide.region_8.9_spmd.sunk.clone | while | flops 1035266 | bytes 11215489 | solution.py:68
  368.7 4.7 %multiply_reduce_fusion = f32[64,8,192]{2,1,0:T(8,128)S(1)} fusion(f32[16,64,8,192]{3,2,1,0:T(8,128)} %get-tuple-element.180, f32[64,8,192]{2,1,0:T(8,128)} %fusion.52, f32[16]{0:T(128)S(1)} %get-tuple-element.638, f32[16,64,8]{2,1,0:T(8,128)S(1)} %copy.36), kind=kLoop, calls=%fused_computation.69 | loop fusion | flops 7766016 | bytes 7110720 | tf_op jit(solution)/shard_map/reduce_sum | solution.py:75
  373.6 19.6 %all_to_all.39 = f32[4,16,8,192]{3,2,1,0:T(8,128)S(1)} all-to-all(f32[4,16,8,192]{3,2,1,0:T(8,128)S(1)} %pad_maximum_fusion.9), channel_id=1, replica_groups=mesh['slides'=2,'rows'=4,'cols'=2,'chan'=2] {'rows'}, dimensions={0} | all-to-all | bytes 786432 | tf_op jit(solution)/shard_map/all_to_all | solution.py:131
  (1559 shorter events, 259.2 us)
Async XLA Ops:
  6.5 9.7 %copy-start = (f32[16,192]{1,0:T(8,128)S(1)}, f32[16,192]{1,0:T(8,128)}, u32[]{:S(2)}) copy-start(f32[16,192]{1,0:T(8,128)} %param.19) | copy-start | bytes 36868
  6.5 24.1 %all-reduce.25.cloned.1.call-start = ((), (), s32[]{:S(2)}) async-start(), calls=%async_computation.3 | async-start | bytes 524288 | tf_op jit(solution)/shard_map/psum | solution.py:97
  9.9 232.8 %all-to-all-start.1 = ((s32[4,1,128]{2,1,0:T(1,128)}), s32[4,1,128]{2,1,0:T(1,128)S(1)}, u32[]{:S(2)}, u32[]{:S(2)}) async-start(s32[4,1,128]{2,1,0:T(1,128)} %reshape.31), calls=%async_computation.1 | async-start | bytes 4096 | tf_op jit(solution)/shard_map/all_to_all | solution.py:121
  212.7 19.5 %copy-start.7 = (f32[16]{0:T(128)S(1)}, f32[16]{0:T(128)}, u32[]{:S(2)}) copy-start(f32[16]{0:T(128)} %get-tuple-element.636) | copy-start | bytes 196
  212.7 19.8 %copy-start.5 = (f32[16,16,32]{0,2,1:T(8,128)S(1)}, f32[16,16,32]{0,2,1:T(8,128)}, u32[]{:S(2)}) copy-start(f32[16,16,32]{0,2,1:T(8,128)} %get-tuple-element.313) | copy-start | bytes 98308
  212.7 20.0 %copy-start.4 = (f32[16,32,192]{2,1,0:T(8,128)S(1)}, f32[16,32,192]{2,1,0:T(8,128)}, u32[]{:S(2)}) copy-start(f32[16,32,192]{2,1,0:T(8,128)} %copy.32) | copy-start | bytes 1179652
  222.7 14.9 %copy-start.3 = (bf16[16,32,192]{2,1,0:T(8,128)(2,1)S(1)}, bf16[16,32,192]{2,1,0:T(8,128)(2,1)}, u32[]{:S(2)}) copy-start(bf16[16,32,192]{2,1,0:T(8,128)(2,1)} %param.16) | copy-start | bytes 589828
  222.7 14.9 %copy-start.10 = (f32[192]{0:T(256)S(1)}, f32[192]{0:T(256)}, u32[]{:S(2)}) copy-start(f32[192]{0:T(256)} %param.25) | copy-start | bytes 2308
  222.7 19.9 %copy-start.9 = (f32[3,3,192]{2,1,0:T(4,128)S(1)}, f32[3,3,192]{2,1,0:T(4,128)}, u32[]{:S(2)}) copy-start(f32[3,3,192]{2,1,0:T(4,128)} %param.23) | copy-start | bytes 20740
  232.2 24.0 %copy-start.11 = (f32[192]{0:T(256)S(1)}, f32[192]{0:T(256)}, u32[]{:S(2)}) copy-start(f32[192]{0:T(256)} %param.24) | copy-start | bytes 2308
  232.7 35.4 %copy-start.8 = (bf16[192,32]{0,1:T(8,128)(2,1)S(1)}, bf16[192,32]{0,1:T(8,128)(2,1)}, u32[]{:S(2)}) copy-start(bf16[192,32]{0,1:T(8,128)(2,1)} %param.22) | copy-start | bytes 36868
  237.6 6.3 %collective-permute-start = (bf16[1,32,192]{2,1,0:T(8,128)(2,1)S(1)}, bf16[1,32,192]{2,1,0:T(8,128)(2,1)S(1)}, u32[]{:S(2)}, u32[]{:S(2)}) collective-permute-start(bf16[1,32,192]{2,1,0:T(8,128)(2,1)S(1)} %get-tuple-element.311), channel_id=1, source_target_pairs={{0,4},{4,8},{8,12},{1,5},{5,9},{9,13},{2,6},{6,10},{10,14},{3,7},{... | collective-permute-start | bytes 36872 | tf_op jit(solution)/shard_map/ppermute | solution.py:29
  241.3 5.6 %collective-permute-start.1 = (bf16[1,32,192]{2,1,0:T(8,128)(2,1)S(1)}, bf16[1,32,192]{2,1,0:T(8,128)(2,1)S(1)}, u32[]{:S(2)}, u32[]{:S(2)}) collective-permute-start(bf16[1,32,192]{2,1,0:T(8,128)(2,1)S(1)} %get-tuple-element.312), channel_id=1, source_target_pairs={{4,0},{8,4},{12,8},{5,1},{9,5},{13,9},{6,2},{10,6},{14,10},{7,3},{... | collective-permute-start | bytes 36872 | tf_op jit(solution)/shard_map/ppermute | solution.py:32
  247.0 4.8 %collective-permute-start.2 = (bf16[18,1,192]{2,1,0:T(2,128)(2,1)S(1)}, bf16[18,1,192]{2,1,0:T(2,128)(2,1)S(1)}, u32[]{:S(2)}, u32[]{:S(2)}) collective-permute-start(bf16[18,1,192]{2,1,0:T(2,128)(2,1)S(1)} %get-tuple-element.307), channel_id=1, source_target_pairs={{0,2},{1,3},{4,6},{5,7},{8,10},{9,11},{12,14},{13,15},{16,18},{17,... | collective-permute-start | bytes 20744 | tf_op jit(solution)/shard_map/ppermute | solution.py:29
  250.4 5.7 %collective-permute-start.3 = (bf16[18,1,192]{2,1,0:T(2,128)(2,1)S(1)}, bf16[18,1,192]{2,1,0:T(2,128)(2,1)S(1)}, u32[]{:S(2)}, u32[]{:S(2)}) collective-permute-start(bf16[18,1,192]{2,1,0:T(2,128)(2,1)S(1)} %get-tuple-element.308), channel_id=1, source_target_pairs={{2,0},{3,1},{6,4},{7,5},{10,8},{11,9},{14,12},{15,13},{18,16},{19,... | collective-permute-start | bytes 20744 | tf_op jit(solution)/shard_map/ppermute | solution.py:32
  257.5 10.5 %all-to-all-start = ((bf16[16,32,192]{2,0,1:T(8,128)(2,1)}), bf16[16,32,192]{2,0,1:T(8,128)(2,1)S(1)}, u32[]{:S(2)}, u32[]{:S(2)}) async-start(bf16[16,32,192]{2,0,1:T(8,128)(2,1)} %copy.34), calls=%async_computation | async-start | bytes 524288 | tf_op jit(solution)/shard_map/all_to_all | solution.py:120
  261.2 25.0 %all-reduce.27.cloned.1.call-start = ((), (), s32[]{:S(2)}) async-start(), calls=%async_computation.4 | async-start | bytes 524288 | tf_op jit(solution)/shard_map/psum | solution.py:79
  268.1 21.3 %copy-start.1 = (bf16[16,4,8,192]{3,2,0,1:T(8,128)(2,1)}, bf16[16,4,8,192]{3,2,0,1:T(8,128)(2,1)S(1)}, u32[]{:S(2)}) copy-start(bf16[16,4,8,192]{3,2,0,1:T(8,128)(2,1)S(1)} %copy.35) | copy-start | bytes 589828
  367.2 6.2 %copy-start.2 = (bf16[16,4,8,192]{3,2,0,1:T(8,128)(2,1)S(1)}, bf16[16,4,8,192]{3,2,0,1:T(8,128)(2,1)}, u32[]{:S(2)}) copy-start(bf16[16,4,8,192]{3,2,0,1:T(8,128)(2,1)} %copy-done.1) | copy-start | bytes 589828
  367.2 26.0 %copy-start.6 = (bf16[16,32,192]{2,1,0:T(8,128)(2,1)S(1)}, bf16[16,32,192]{2,1,0:T(8,128)(2,1)}, u32[]{:S(2)}) copy-start(bf16[16,32,192]{2,1,0:T(8,128)(2,1)} %param.17) | copy-start | bytes 589828
Sparse Core Ops, SparseCore 0:
  9.7 20.9 all-reduce.24
  269.1 17.0 all-reduce.26
